TPU v7x, 256 devices: a whole 4x4x8 slice. The times are simulated.
256 devices in a mesh: file: 8 (over x, core), blk: 32 (over z, y).
Axes of the slice: x: 4, y: 4, z: 8, core: 2. Of those that a mesh axis runs over, the one named last changes fastest.
Arguments:
- ctx_keys: bfloat16 [32768, 256], P(('file', 'blk')), parts along dimension 0, may hold values from -4 to 4
- ctx_values: bfloat16 [32768, 256], P(('file', 'blk')), parts along dimension 0, may hold values from -6 to 6
- middle_queries: bfloat16 [32768, 1792], P(('file', 'blk')), parts along dimension 0, may hold values from -40 to 40
- span_keys: bfloat16 [32768, 256], P(('file', 'blk')), parts along dimension 0, may hold values from -6 to 6
- span_values: bfloat16 [32768, 256], P(('file', 'blk')), parts along dimension 0, may hold values from -6 to 6
- span_len: int32 [256], P(('file', 'blk')), parts along dimension 0, may hold values from 36 to 128, as said below
- commit_pos: int32 [256, 2, 16], P(('file', 'blk')), parts along dimension 0, may hold values from 4 to 127, as said below
- commit_emb: bfloat16 [256, 2, 16, 3584], P(('file', 'blk')), parts along dimension 0, may hold values from -6 to 6
- w_key: bfloat16 [3584, 256], replicated, may hold values from -0.09375 to 0.09375
- w_value: bfloat16 [3584, 256], replicated, may hold values from -0.09375 to 0.09375
Outputs:
- span_out: bfloat16 [2, 32768, 1792], P(None, ('file', 'blk')), parts along dimension 1
There are 8 independent parts, one for each index of `file`. A program takes and returns all parts, laid end to end along the dimension named above; an argument that names none is the same for every part. Nothing has to cross between parts.
Inputs may be any that keep to these rules, and one draw needn't show every extreme that they name: `span_len`: some device's span fills all 128 slots in every draw. `commit_pos`: each device commits exactly 16 slots a step; a device's committed slots are distinct over all steps and lie below that device's span length.
All inputs are finite; a program needn't handle non-finite values.
Results may differ from a plain program's by a relative error of at most 0.0067.
Values may be sent and summed in bfloat16 or wider, within the bound.
No kernel may reach another device: no remote copies, remote signals or barrier semaphores. Data moves between devices by JAX's collectives and lax.ppermute only.
A program may use at most 256 MiB of HBM per device.

v0:
```python
import math
import jax
import jax.numpy as jnp
from jax import lax
from jax.sharding import PartitionSpec as P

HEAD_WIDTH = 128
KEY_VALUE_HEADS = 2
STEPS = 2
QUERY_PER_KEY = 7


def attend_piece(carried, heads_of_queries, key_matrix, value_matrix, live_keys):
    row_max, row_sum, weighted = carried
    row_count = key_matrix.shape[0]
    heads_of_keys = key_matrix.reshape(row_count, KEY_VALUE_HEADS, HEAD_WIDTH)
    heads_of_values = value_matrix.reshape(row_count, KEY_VALUE_HEADS, HEAD_WIDTH)
    scores = jnp.einsum(
        "sgrd,kgd->gsrk", heads_of_queries, heads_of_keys, preferred_element_type=jnp.float32
    ) / math.sqrt(HEAD_WIDTH)
    scores = jnp.where(live_keys[None, None, None, :], scores, -jnp.inf)
    new_max = jnp.maximum(row_max, jnp.max(scores, axis=-1))
    expw = jnp.exp(scores - new_max[..., None])
    row_sum = jnp.sum(expw, axis=-1)
    weighted = jnp.einsum(
        "gsrk,kgd->gsrd",
        expw.astype(jnp.bfloat16),
        heads_of_values,
        preferred_element_type=jnp.float32,
    )
    return (new_max, row_sum, weighted)


def per_device(
    ctx_keys,
    ctx_values,
    middle_queries,
    span_keys,
    span_values,
    span_len,
    commit_pos,
    commit_emb,
    w_key,
    w_value,
):
    local_rows = middle_queries.shape[0]
    slots = jnp.arange(local_rows, dtype=jnp.int32)
    live_here = slots < span_len[0]
    span_flags = live_here.astype(jnp.bfloat16)
    heads_of_queries = middle_queries.reshape(
        local_rows, KEY_VALUE_HEADS, QUERY_PER_KEY, HEAD_WIDTH
    )
    starting = (
        jnp.full((KEY_VALUE_HEADS, local_rows, QUERY_PER_KEY), -1e30, jnp.float32),
        jnp.zeros((KEY_VALUE_HEADS, local_rows, QUERY_PER_KEY), jnp.float32),
        jnp.zeros((KEY_VALUE_HEADS, local_rows, QUERY_PER_KEY, HEAD_WIDTH), jnp.float32),
    )
    keys_now = span_keys
    values_now = span_values
    committed = jnp.zeros((local_rows,), bool)
    attention_outputs = []
    for number in range(STEPS):
        embedded = commit_emb[0, number]
        new_keys = jnp.dot(embedded, w_key, preferred_element_type=jnp.float32).astype(jnp.bfloat16)
        new_values = jnp.dot(embedded, w_value, preferred_element_type=jnp.float32).astype(
            jnp.bfloat16
        )
        slot_ids = commit_pos[0, number]
        committed = committed | jnp.any(slots[:, None] == slot_ids[None, :], axis=1)
        active = live_here & ~committed
        keys_now = keys_now.at[slot_ids].set(new_keys)
        values_now = values_now.at[slot_ids].set(new_values)
        joined_keys = jnp.concatenate([ctx_keys, keys_now])
        joined_values = jnp.concatenate([ctx_values, values_now])
        joined_flags = jnp.concatenate([jnp.ones((ctx_keys.shape[0],), jnp.bfloat16), span_flags])
        row_max, row_sum, weighted = attend_piece(
            starting,
            heads_of_queries,
            lax.all_gather(joined_keys, "blk", axis=0, tiled=True),
            lax.all_gather(joined_values, "blk", axis=0, tiled=True),
            lax.all_gather(joined_flags, "blk", axis=0, tiled=True) > 0.5,
        )
        attention_output = (
            (weighted / row_sum[..., None])
            .transpose(1, 0, 2, 3)
            .reshape(local_rows, KEY_VALUE_HEADS * QUERY_PER_KEY * HEAD_WIDTH)
        )
        attention_outputs.append(
            jnp.where(active[:, None], attention_output, 0.0).astype(jnp.bfloat16)
        )
    return jnp.stack(attention_outputs)


def solution(mesh):
    in_specs = (
        P(("file", "blk"), None),
        P(("file", "blk"), None),
        P(("file", "blk"), None),
        P(("file", "blk"), None),
        P(("file", "blk"), None),
        P(("file", "blk")),
        P(("file", "blk"), None, None),
        P(("file", "blk"), None, None, None),
        P(),
        P(),
    )
    out_specs = P(None, ("file", "blk"), None)
    return jax.shard_map(
        per_device, mesh=mesh, in_specs=in_specs, out_specs=out_specs, check_vma=False
    )
```

profile of v0, /device:TPU:2, one launch (start us, length us, event | category | flops | bytes accessed | tf_op | source)
XLA Modules:
  0.0 381.8 jit_solution(502001056477325090)
XLA Ops:
  6.5 1.0 copy.77
  7.5 0.8 copy.78
  8.4 1.2 convolution_convert_fusion.3
  9.6 1.3 convolution_convert_fusion.1
  10.9 0.8 fusion.35
  11.6 0.7 scatter_fusion
  12.4 0.7 scatter_fusion.2
  13.1 1.5 pad_maximum_fusion.4
  14.7 0.7 all-gather.10.cloned.1.call-update
  15.5 1.9 convolution_convert_fusion.2
  17.4 0.7 scatter_fusion.1
  18.1 1.9 convolution_convert_fusion
  20.1 0.7 scatter_fusion.3
  20.8 1.5 pad_maximum_fusion.2
  22.9 0.8 slice_bitcast_fusion
  24.5 0.5 not_and_fusion.1
  25.1 46.2 %all-gather = bf16[32,1,256]{2,1,0:T(2,128)(2,1)S(1)} all-gather(bf16[1,1,256]{2,1,0:T(2,128)(2,1)S(1)} %reshape.208), channel_id=1, replica_groups=mesh['file'=8,'blk'=32] {'blk'}, dimensions={0}, use_global_device_ids=true | all-gather | bytes 16896 | tf_op jit(solution)/shard_map/all_gather | solution.py:81
  71.5 1.3 copy.46
  72.7 26.9 %all-gather.6.cloned.1.call-done = bf16[8192,256]{1,0:T(8,128)(2,1)} async-done(((bf16[256,256]{1,0:T(8,128)(2,1)}), bf16[8192,256]{1,0:T(8,128)(2,1)}) %all-gather.6.cloned.1.call-update) | async-done | bytes 4194320 | tf_op jit(solution)/shard_map/all_gather | solution.py:79
  99.6 6.4 %copy.45 = bf16[8192,256]{0,1:T(8,128)(2,1)} copy(bf16[8192,256]{1,0:T(8,128)(2,1)} %all-gather.6.cloned.1.call-done) | data formatting | bytes 8388608 | tf_op jit(solution)/shard_map/all_gather | solution.py:79
  106.0 24.6 %bitcast_reduce_fusion.1 = (f32[2,128,7]{1,2,0:T(8,128)S(1)}, f32[2,8192,128,7]{2,1,3,0:T(8,128)}) fusion(pred[8192]{0:T(1024)(128)(4,1)S(1)} %reshape.211, bf16[8192,2,128,1]{0,2,3,1:T(8,128)(2,1)} %bitcast.95, bf16[128,2,7,128]{0,3,2,1:T(8,128)(2,1)S(1)} %bitcast.99), kind=kOutput, calls=%fused_computation.8 | convolution fusion | flops 3802134784 | bytes 63388672 | tf_op jit(solution)/shard_map/sgrd,kgd->gsrk/dot_general | solution.py:18
  130.6 50.8 %all-gather.10.cloned.1.call-done = bf16[8192,256]{1,0:T(8,128)(2,1)} async-done(((bf16[256,256]{1,0:T(8,128)(2,1)}), bf16[8192,256]{1,0:T(8,128)(2,1)}) %all-gather.10.cloned.1.call-update) | async-done | bytes 4194320 | tf_op jit(solution)/shard_map/all_gather | solution.py:79
  181.3 6.4 %copy.52 = bf16[8192,256]{0,1:T(8,128)(2,1)} copy(bf16[8192,256]{1,0:T(8,128)(2,1)} %all-gather.10.cloned.1.call-done) | data formatting | bytes 8388608 | tf_op jit(solution)/shard_map/all_gather | solution.py:79
  187.7 49.4 %fusion.2 = (f32[2,128,7]{1,2,0:T(8,128)S(1)}, f32[2,128,7]{1,2,0:T(8,128)S(1)}, f32[2,8192,128,7]{2,1,3,0:T(8,128)}) fusion(f32[2,8192,128,7]{2,1,3,0:T(8,128)} %get-tuple-element.18, f32[2,128,7]{1,2,0:T(8,128)S(1)} %broadcast_maximum_fusion.1, pred[8192]{0:T(1024)(128)(4,1)S(1)} %reshape.211, bf16[8192,2,128,1]{0,2,3,1:T(8,128)(2,1)} %bitcast.96, ...), kind=kOutput, calls=%fused_computation.12 | convolution fusion | flops 3860853248 | bytes 122123264 | tf_op jit(solution)/shard_map/sgrd,kgd->gsrk/dot_general | solution.py:18
  237.1 26.0 %all-gather.8.cloned.1.call-done = bf16[8192,256]{1,0:T(8,128)(2,1)} async-done(((bf16[256,256]{1,0:T(8,128)(2,1)}), bf16[8192,256]{1,0:T(8,128)(2,1)}) %all-gather.8.cloned.1.call-update) | async-done | bytes 4194320 | tf_op jit(solution)/shard_map/all_gather | solution.py:80
  263.0 6.4 %copy.49 = bf16[8192,256]{0,1:T(8,128)(2,1)} copy(bf16[8192,256]{1,0:T(8,128)(2,1)} %all-gather.8.cloned.1.call-done) | data formatting | bytes 8388608 | tf_op jit(solution)/shard_map/all_gather | solution.py:80
  269.4 22.8 %fusion.21 = bf16[128,2,7,128]{0,3,2,1:T(8,128)(2,1)S(1)} fusion(bf16[8192,2,128,1]{0,2,3,1:T(8,128)(2,1)} %bitcast.98, f32[2,8192,128,7]{2,1,3,0:T(8,128)} %get-tuple-element.18, f32[2,128,7]{1,2,0:T(8,128)S(1)} %broadcast_maximum_fusion.1, pred[8192]{0:T(1024)(128)(4,1)S(1)} %reshape.211, f32[128,2,7]{0,2,1:T(8,128)S(1)} %bitcast.104), kind=kOutput, calls=%fused_computation.23 | convolution fusion | flops 3817275392 | bytes 63395840 | tf_op jit(solution)/shard_map/gsrk,kgd->gsrd/dot_general | solution.py:25
  292.5 19.4 %fusion.4 = f32[2,128,7]{1,2,0:T(8,128)S(1)} fusion(f32[2,8192,128,7]{2,1,3,0:T(8,128)} %get-tuple-element.19, f32[2,128,7]{1,2,0:T(8,128)S(1)} %broadcast_maximum_fusion, pred[8192]{0:T(1024)(128)(4,1)S(1)} %reshape.211), kind=kLoop, calls=%fused_computation.14 | loop fusion | flops 58718464 | bytes 58742784 | tf_op jit(solution)/shard_map/reduce_sum | solution.py:24
  311.9 32.7 %all-gather.12.cloned.1.call-done = bf16[8192,256]{1,0:T(8,128)(2,1)} async-done(((bf16[256,256]{1,0:T(8,128)(2,1)}), bf16[8192,256]{1,0:T(8,128)(2,1)}) %all-gather.12.cloned.1.call-update) | async-done | bytes 4194320 | tf_op jit(solution)/shard_map/all_gather | solution.py:80
  344.6 6.4 %copy.55 = bf16[8192,256]{0,1:T(8,128)(2,1)} copy(bf16[8192,256]{1,0:T(8,128)(2,1)} %all-gather.12.cloned.1.call-done) | data formatting | bytes 8388608 | tf_op jit(solution)/shard_map/all_gather | solution.py:80
  351.0 22.7 %fusion.18 = bf16[128,2,7,128]{0,3,2,1:T(8,128)(2,1)S(1)} fusion(bf16[8192,2,128,1]{0,2,3,1:T(8,128)(2,1)} %bitcast.97, f32[2,8192,128,7]{2,1,3,0:T(8,128)} %get-tuple-element.19, f32[2,128,7]{1,2,0:T(8,128)S(1)} %broadcast_maximum_fusion, pred[8192]{0:T(1024)(128)(4,1)S(1)} %reshape.211, f32[128,2,7]{0,2,1:T(8,128)S(1)} %bitcast.103), kind=kOutput, calls=%fused_computation.22 | convolution fusion | flops 3817275392 | bytes 63395840 | tf_op jit(solution)/shard_map/gsrk,kgd->gsrd/dot_general | solution.py:25
  374.2 1.0 pad_maximum_fusion
  (29 shorter events, 1.8 us)
Async XLA Ops:
  6.5 1.8 copy-start
  6.5 93.1 %all-gather.6.cloned.1.call-start = ((), (), s32[]{:S(2)}) async-start(), calls=%async_computation | async-start | bytes 4325376 | tf_op jit(solution)/shard_map/all_gather | solution.py:79
  14.7 166.7 %all-gather.10.cloned.1.call-start = ((), (), s32[]{:S(2)}) async-start(), calls=%async_computation.2 | async-start | bytes 4325376 | tf_op jit(solution)/shard_map/all_gather | solution.py:79
  15.4 247.6 %all-gather.8.cloned.1.call-start = ((), (), s32[]{:S(2)}) async-start(), calls=%async_computation.1 | async-start | bytes 4325376 | tf_op jit(solution)/shard_map/all_gather | solution.py:80
  22.4 322.3 %all-gather.12.cloned.1.call-start = ((), (), s32[]{:S(2)}) async-start(), calls=%async_computation.3 | async-start | bytes 4325376 | tf_op jit(solution)/shard_map/all_gather | solution.py:80
  292.5 82.8 %copy-start.1 = (bf16[3584,256]{1,0:T(8,128)(2,1)S(1)}, bf16[3584,256]{1,0:T(8,128)(2,1)}, u32[]{:S(2)}) copy-start(bf16[3584,256]{1,0:T(8,128)(2,1)} %param.18) | copy-start | bytes 5505028
  311.9 62.0 %copy-start.3 = (pred[128]{0:T(512)(128)(4,1)S(1)}, pred[128]{0:T(512)(128)(4,1)}, u32[]{:S(2)}) copy-start(pred[128]{0:T(512)(128)(4,1)} %get-tuple-element.15) | copy-start | bytes 388
  311.9 62.2 %copy-start.2 = (pred[128]{0:T(512)(128)(4,1)S(1)}, pred[128]{0:T(512)(128)(4,1)}, u32[]{:S(2)}) copy-start(pred[128]{0:T(512)(128)(4,1)} %get-tuple-element.16) | copy-start | bytes 388
Sparse Core Ops, SparseCore 0:
  14.8 84.7 all-gather.5
  102.2 79.0 all-gather.9
  183.9 79.0 all-gather.7
  265.5 79.0 all-gather.11
where the time goes:
time: 383 us; the launch traced here: 382 us
  waiting for transfers between devices  138 us (36%)
  matrix products  126 us (33%)
  blocking collectives  46.2 us (12%)
  local copies, waits for them, and re-layouts  32.7 us (9%)
  other arithmetic  25.4 us (7%)
  between operations  13.9 us (4%)
    all_gather x2, waiting for transfers between devices, per_device(): lax.all_gather(joined_keys, 'blk', axis=0, tiled=True)  77.6 us
    dot_general x2, matrix products, attend_piece(): jnp.einsum('sgrd,kgd->gsrk', heads_of_queries, heads_of_keys, preferred_e...  73.9 us
    all_gather x2, waiting for transfers between devices, per_device(): lax.all_gather(joined_values, 'blk', axis=0, tiled=True)  58.7 us
    all_gather x1, blocking collectives, per_device(): lax.all_gather(joined_flags, 'blk', axis=0, tiled=True) > 0.5  46.2 us
    dot_general x2, matrix products, attend_piece(): jnp.einsum('gsrk,kgd->gsrd', expw.astype(jnp.bfloat16), heads_of_values,...  45.5 us
    reduce_sum x1, other arithmetic, attend_piece(): row_sum = jnp.sum(expw, axis=-1)  19.4 us
    all_gather x2, local copies, waits for them, and re-layouts, per_device(): lax.all_gather(joined_keys, 'blk', axis=0, tiled=True)  12.7 us
    all_gather x2, local copies, waits for them, and re-layouts, per_device(): lax.all_gather(joined_values, 'blk', axis=0, tiled=True)  12.7 us
  transfers between devices with their start and end apart: 4, of which 4 were waited for; matrix products, arithmetic and copies ran while one was open for 38% of the time, Pallas kernels for 0%

commit v1 on v0

--- a/solution.py
+++ b/solution.py
@@ -8,6 +8,11 @@
 KEY_VALUE_HEADS = 2
 STEPS = 2
 QUERY_PER_KEY = 7
+
+
+def all_by_exchange(x, axis, d):
+    outgoing = jnp.stack([x] * lax.axis_size(axis))
+    return jnp.concatenate(lax.all_to_all(outgoing, axis, 0, 0), axis=d)
 
 
 def attend_piece(carried, heads_of_queries, key_matrix, value_matrix, live_keys):
@@ -77,7 +82,7 @@
             starting,
             heads_of_queries,
             lax.all_gather(joined_keys, "blk", axis=0, tiled=True),
-            lax.all_gather(joined_values, "blk", axis=0, tiled=True),
+            all_by_exchange(joined_values, "blk", 0),
             lax.all_gather(joined_flags, "blk", axis=0, tiled=True) > 0.5,
         )
         attention_output = (

time: 383 us -> 433 us (1.13); the launches traced: 382 us -> 427 us
  blocking collectives: 46.2 us -> 148 us
  waiting for transfers between devices: 138 us -> 44 us
  local copies, waits for them, and re-layouts: 32.7 us -> 52.9 us
  starting transfers between devices: 0.12 us -> 17.6 us
    all_gather x1, blocking collectives: 46.2 us -> 148 us  [per_device(): lax.all_gather(joined_flags, 'blk', axis=0, tiled=True) > 0.5]
    all_gather x2 -> x0, waiting for transfers between devices: 58.7 us -> none  [per_device(): lax.all_gather(joined_values, 'blk', axis=0, tiled=True)]
    all_gather x2, waiting for transfers between devices: 77.6 us -> 43.2 us  [per_device(): lax.all_gather(joined_keys, 'blk', axis=0, tiled=True)]
    another operation x0 -> x4, local copies, waits for them, and re-layouts: none -> 19.7 us  [the longest x2 14.8 us: attend_piece(): value_matrix.reshape(row_count, KEY_VALUE_HEADS, HEAD_WIDTH)]
    all_to_all x0 -> x2, starting transfers between devices: none -> 17.6 us  [all_by_exchange(): return jnp.concatenate(lax.all_to_all(outgoing, axis, 0, 0), axis=d)]
    all_to_all x0 -> x2, local copies, waits for them, and re-layouts: none -> 13 us  [all_by_exchange(): return jnp.concatenate(lax.all_to_all(outgoing, axis, 0, 0), axis=d)]
    all_gather x2 -> x0, local copies, waits for them, and re-layouts: 12.7 us -> none  [per_device(): lax.all_gather(joined_values, 'blk', axis=0, tiled=True)]
  transfers between devices with their start and end apart: 4 -> 4, of which waited for: 4 -> 1; matrix products, arithmetic and copies ran while one was open for 38% -> 32% of each run, Pallas kernels for 0% -> 0%
where the time goes in v1:
time: 433 us; the launch traced here: 427 us
  blocking collectives  148 us (34%)
  matrix products  126 us (29%)
  local copies, waits for them, and re-layouts  52.9 us (12%)
  waiting for transfers between devices  44 us (10%)
  other arithmetic  24.6 us (6%)
  starting transfers between devices  17.6 us (4%)
  between operations  14.3 us (3%)
    all_gather x1, blocking collectives, per_device(): lax.all_gather(joined_flags, 'blk', axis=0, tiled=True) > 0.5  148 us
    dot_general x2, matrix products, attend_piece(): jnp.einsum('sgrd,kgd->gsrk', heads_of_queries, heads_of_keys, preferred_e...  74.1 us
    dot_general x2, matrix products, attend_piece(): jnp.einsum('gsrk,kgd->gsrd', expw.astype(jnp.bfloat16), heads_of_values,...  45.3 us
    all_gather x2, waiting for transfers between devices, per_device(): lax.all_gather(joined_keys, 'blk', axis=0, tiled=True)  43.2 us
    reduce_sum x1, other arithmetic, attend_piece(): row_sum = jnp.sum(expw, axis=-1)  19.2 us
    all_to_all x2, starting transfers between devices, all_by_exchange(): return jnp.concatenate(lax.all_to_all(outgoing, axis, 0, 0), axis=d)  17.6 us
    another operation x2, local copies, waits for them, and re-layouts, attend_piece(): value_matrix.reshape(row_count, KEY_VALUE_HEADS, HEAD_WIDTH)  14.8 us
    all_to_all x2, local copies, waits for them, and re-layouts, all_by_exchange(): return jnp.concatenate(lax.all_to_all(outgoing, axis, 0, 0), axis=d)  13 us
  transfers between devices with their start and end apart: 4, of which 1 were waited for; matrix products, arithmetic and copies ran while one was open for 32% of the time, Pallas kernels for 0%

profile of v1, /device:TPU:2, one launch (start us, length us, event | category | flops | bytes accessed | tf_op | source)
XLA Modules:
  0.0 426.9 jit_solution(11732396096783201669)
XLA Ops:
  6.5 1.0 copy.81
  7.5 0.8 copy.82
  8.4 1.2 convolution_convert_fusion.3
  9.6 1.3 convolution_convert_fusion.1
  10.9 0.8 fusion.45
  12.4 0.7 scatter_fusion.2
  13.1 1.5 pad_maximum_fusion.4
  14.7 1.9 convolution_convert_fusion.2
  16.6 0.7 scatter_fusion.1
  17.3 1.9 convolution_convert_fusion
  19.3 0.7 scatter_fusion.3
  20.0 0.9 pad_maximum_fusion.2
  21.0 2.4 stack.6
  23.4 11.6 %all-to-all-start = ((bf16[32,256,256]{1,2,0:T(8,128)(2,1)}), bf16[32,256,256]{1,2,0:T(8,128)(2,1)}, u32[]{:S(2)}, u32[]{:S(2)}) async-start(bf16[32,256,256]{1,2,0:T(8,128)(2,1)} %stack.6), calls=%async_computation | async-start | bytes 8388608 | tf_op jit(solution)/shard_map/all_to_all | solution.py:15
  36.4 0.8 slice_bitcast_fusion
  38.0 147.8 %all-gather = bf16[32,1,256]{2,1,0:T(2,128)(2,1)S(1)} all-gather(bf16[1,1,256]{2,1,0:T(2,128)(2,1)S(1)} %reshape.204), channel_id=1, replica_groups=mesh['file'=8,'blk'=32] {'blk'}, dimensions={0}, use_global_device_ids=true | all-gather | bytes 16896 | tf_op jit(solution)/shard_map/all_gather | solution.py:86
  185.9 1.3 copy.48
  187.3 2.5 stack.7
  189.8 6.0 %all-to-all-start.1 = ((bf16[32,256,256]{1,2,0:T(8,128)(2,1)}), bf16[32,256,256]{1,2,0:T(8,128)(2,1)}, u32[]{:S(2)}, u32[]{:S(2)}) async-start(bf16[32,256,256]{1,2,0:T(8,128)(2,1)} %stack.7), calls=%async_computation.1 | async-start | bytes 8388608 | tf_op jit(solution)/shard_map/all_to_all | solution.py:15
  195.8 6.5 %copy.52 = bf16[32,256,256]{1,0,2:T(8,128)(2,1)} copy(bf16[32,256,256]{1,2,0:T(8,128)(2,1)} %all-to-all-done) | data formatting | bytes 8388608 | tf_op jit(solution)/shard_map/all_to_all | solution.py:15
  202.3 7.4 %reshape.209 = bf16[8192,2,128,1]{0,2,1,3:T(8,128)(2,1)} reshape(bf16[32,256,256]{1,0,2:T(8,128)(2,1)} %copy.52) | data formatting | bytes 8388608 | tf_op jit(solution)/shard_map/reshape;reshape | solution.py:22
  209.7 6.3 %copy.47 = bf16[8192,256]{0,1:T(8,128)(2,1)} copy(bf16[8192,256]{1,0:T(8,128)(2,1)} %all-gather.4.cloned.1.call-done) | data formatting | bytes 8388608 | tf_op jit(solution)/shard_map/all_gather | solution.py:84
  216.0 24.8 %bitcast_reduce_fusion.1 = (f32[2,128,7]{1,2,0:T(8,128)S(1)}, f32[2,8192,128,7]{2,1,3,0:T(8,128)}) fusion(pred[8192]{0:T(1024)(128)(4,1)S(1)} %reshape.207, bf16[8192,2,128,1]{0,2,3,1:T(8,128)(2,1)} %bitcast.101, bf16[128,2,7,128]{0,3,2,1:T(8,128)(2,1)S(1)} %bitcast.103), kind=kOutput, calls=%fused_computation.8 | convolution fusion | flops 3802134784 | bytes 63388672 | tf_op jit(solution)/shard_map/sgrd,kgd->gsrk/dot_general | solution.py:23
  240.8 43.2 %all-gather.6.cloned.1.call-done = bf16[8192,256]{1,0:T(8,128)(2,1)} async-done(((bf16[256,256]{1,0:T(8,128)(2,1)}), bf16[8192,256]{1,0:T(8,128)(2,1)}) %all-gather.6.cloned.1.call-update) | async-done | bytes 4194320 | tf_op jit(solution)/shard_map/all_gather | solution.py:84
  284.1 6.4 %copy.55 = bf16[8192,256]{0,1:T(8,128)(2,1)} copy(bf16[8192,256]{1,0:T(8,128)(2,1)} %all-gather.6.cloned.1.call-done) | data formatting | bytes 8388608 | tf_op jit(solution)/shard_map/all_gather | solution.py:84
  290.5 49.3 %fusion.2 = (f32[2,128,7]{1,2,0:T(8,128)S(1)}, f32[2,128,7]{1,2,0:T(8,128)S(1)}, f32[2,8192,128,7]{2,1,3,0:T(8,128)}) fusion(f32[2,8192,128,7]{2,1,3,0:T(8,128)} %get-tuple-element.18, f32[2,128,7]{1,2,0:T(8,128)S(1)} %broadcast_maximum_fusion.1, pred[8192]{0:T(1024)(128)(4,1)S(1)} %reshape.207, bf16[8192,2,128,1]{0,2,3,1:T(8,128)(2,1)} %bitcast.102, ...), kind=kOutput, calls=%fused_computation.12 | convolution fusion | flops 3860853248 | bytes 122123264 | tf_op jit(solution)/shard_map/sgrd,kgd->gsrk/dot_general | solution.py:23
  339.8 22.6 %fusion.29 = bf16[128,2,7,128]{0,3,2,1:T(8,128)(2,1)S(1)} fusion(f32[2,8192,128,7]{2,1,3,0:T(8,128)} %get-tuple-element.18, f32[2,128,7]{1,2,0:T(8,128)S(1)} %broadcast_maximum_fusion.1, pred[8192]{0:T(1024)(128)(4,1)S(1)} %reshape.207, bf16[8192,2,128,1]{0,2,1,3:T(8,128)(2,1)} %reshape.209, f32[128,2,7]{0,2,1:T(8,128)S(1)} %bitcast.108), kind=kOutput, calls=%fused_computation.25 | convolution fusion | flops 3817275392 | bytes 63395840 | tf_op jit(solution)/shard_map/gsrk,kgd->gsrd/dot_general | solution.py:30
  362.6 6.5 %copy.59 = bf16[32,256,256]{1,0,2:T(8,128)(2,1)} copy(bf16[32,256,256]{1,2,0:T(8,128)(2,1)} %all-to-all-done.1) | data formatting | bytes 8388608 | tf_op jit(solution)/shard_map/all_to_all | solution.py:15
  369.1 7.4 %reshape.211 = bf16[8192,2,128,1]{0,2,1,3:T(8,128)(2,1)} reshape(bf16[32,256,256]{1,0,2:T(8,128)(2,1)} %copy.59) | data formatting | bytes 8388608 | tf_op jit(solution)/shard_map/reshape;reshape | solution.py:22
  376.5 19.2 %fusion.4 = f32[2,128,7]{1,2,0:T(8,128)S(1)} fusion(f32[2,8192,128,7]{2,1,3,0:T(8,128)} %get-tuple-element.19, f32[2,128,7]{1,2,0:T(8,128)S(1)} %broadcast_maximum_fusion, pred[8192]{0:T(1024)(128)(4,1)S(1)} %reshape.207), kind=kLoop, calls=%fused_computation.14 | loop fusion | flops 58718464 | bytes 58742784 | tf_op jit(solution)/shard_map/reduce_sum | solution.py:29
  395.7 22.8 %fusion.24 = bf16[128,2,7,128]{0,3,2,1:T(8,128)(2,1)S(1)} fusion(f32[2,8192,128,7]{2,1,3,0:T(8,128)} %get-tuple-element.19, f32[2,128,7]{1,2,0:T(8,128)S(1)} %broadcast_maximum_fusion, pred[8192]{0:T(1024)(128)(4,1)S(1)} %reshape.207, bf16[8192,2,128,1]{0,2,1,3:T(8,128)(2,1)} %reshape.211, f32[128,2,7]{0,2,1:T(8,128)S(1)} %bitcast.107), kind=kOutput, calls=%fused_computation.24 | convolution fusion | flops 3817275392 | bytes 63395840 | tf_op jit(solution)/shard_map/gsrk,kgd->gsrd/dot_general | solution.py:30
  419.0 1.0 pad_maximum_fusion
  (33 shorter events, 3.4 us)
Async XLA Ops:
  6.5 1.8 copy-start
  6.5 203.1 %all-gather.4.cloned.1.call-start = ((), (), s32[]{:S(2)}) async-start(), calls=%async_computation.2 | async-start | bytes 4325376 | tf_op jit(solution)/shard_map/all_gather | solution.py:84
  23.4 163.9 %all-to-all-start = ((bf16[32,256,256]{1,2,0:T(8,128)(2,1)}), bf16[32,256,256]{1,2,0:T(8,128)(2,1)}, u32[]{:S(2)}, u32[]{:S(2)}) async-start(bf16[32,256,256]{1,2,0:T(8,128)(2,1)} %stack.6), calls=%async_computation | async-start | bytes 8388608 | tf_op jit(solution)/shard_map/all_to_all | solution.py:15
  35.0 249.1 %all-gather.6.cloned.1.call-start = ((), (), s32[]{:S(2)}) async-start(), calls=%async_computation.3 | async-start | bytes 4325376 | tf_op jit(solution)/shard_map/all_gather | solution.py:84
  189.8 172.9 %all-to-all-start.1 = ((bf16[32,256,256]{1,2,0:T(8,128)(2,1)}), bf16[32,256,256]{1,2,0:T(8,128)(2,1)}, u32[]{:S(2)}, u32[]{:S(2)}) async-start(bf16[32,256,256]{1,2,0:T(8,128)(2,1)} %stack.7), calls=%async_computation.1 | async-start | bytes 8388608 | tf_op jit(solution)/shard_map/all_to_all | solution.py:15
  395.7 24.3 %copy-start.1 = (bf16[3584,256]{1,0:T(8,128)(2,1)S(1)}, bf16[3584,256]{1,0:T(8,128)(2,1)}, u32[]{:S(2)}) copy-start(bf16[3584,256]{1,0:T(8,128)(2,1)} %param.18) | copy-start | bytes 5505028
  395.7 23.0 %copy-start.3 = (pred[128]{0:T(512)(128)(4,1)S(1)}, pred[128]{0:T(512)(128)(4,1)}, u32[]{:S(2)}) copy-start(pred[128]{0:T(512)(128)(4,1)} %get-tuple-element.15) | copy-start | bytes 388
  395.7 23.2 %copy-start.2 = (pred[128]{0:T(512)(128)(4,1)S(1)}, pred[128]{0:T(512)(128)(4,1)}, u32[]{:S(2)}) copy-start(pred[128]{0:T(512)(128)(4,1)} %get-tuple-element.16) | copy-start | bytes 388
Sparse Core Ops, SparseCore 0:
  14.8 130.4 all-gather.3
  147.9 136.1 all-gather.5
